TPU v7x, 32 devices: a whole 2x2x4 slice. The times are simulated.
32 devices in a mesh: space: 4 (over y, x), exc: 8 (over z, core).
Axes of the slice: x: 2, y: 2, z: 4, core: 2. Of those that a mesh axis runs over, the one named last changes fastest.
Arguments:
- coeff: float32 [64, 256, 4096], P('space', None, 'exc'), may hold values from -6 to 6
- factors: float32 [4, 64, 256, 512], P(None, 'space', 'exc'), may hold values from -0.25 to 0.25
Outputs:
- applied: float32 [64, 256, 4096], P('space', None, 'exc')
All inputs are finite; a program needn't handle non-finite values.
Results may differ from a plain program's by a relative error of at most 0.0003.
Values sent between devices are 32-bit elements; how exact they have to be, the bound alone decides.
A program may use at most 128 MiB of HBM per device.

v0:
```python
import jax
import jax.numpy as jnp
from jax import lax
from jax.sharding import PartitionSpec as P

BITS = 6
LEVELS = 4


def paired(state, bit):
    count = state.shape[0]
    stride = 1 << bit
    shaped = state.reshape(count // (2 * stride), 2, stride, state.shape[1], state.shape[2])
    return shaped[:, ::-1].reshape(state.shape)


def contract(rows, state, other):
    stacked = jnp.concatenate([state, other], axis=1)
    return jnp.einsum(
        "brk,bke->bre",
        rows,
        stacked,
        precision=lax.Precision.HIGHEST,
        preferred_element_type=jnp.float32,
    )


def level_product(rows_dev, state, other):
    return contract(lax.all_gather(rows_dev, "exc", axis=1, tiled=True), state, other)


def regroup(state, groups):
    shaped = state.reshape(groups, state.shape[0] // groups, state.shape[1], state.shape[2])
    return lax.all_to_all(shaped, "space", split_axis=0, concat_axis=0, tiled=True).reshape(
        state.shape
    )


def restore(state, groups):
    shaped = state.reshape(groups, state.shape[0] // groups, state.shape[1], state.shape[2])
    return lax.all_to_all(shaped, "space", split_axis=0, concat_axis=0, tiled=True).reshape(
        state.shape
    )


def body(coeff, factors):
    blocks_dev = coeff.shape[0]
    local_bits = blocks_dev.bit_length() - 1
    groups = lax.axis_size("space")
    group_bits = groups.bit_length() - 1
    first_bit = BITS - LEVELS
    cross_start = min(LEVELS, max(0, local_bits - first_bit))
    level_rows = [factors[level] for level in range(LEVELS)]
    moved = factors[cross_start:]
    shaped = moved.reshape(
        moved.shape[0], groups, blocks_dev // groups, moved.shape[2], moved.shape[3]
    )
    shaped = lax.all_to_all(shaped, "space", split_axis=1, concat_axis=1, tiled=True).reshape(
        moved.shape
    )
    level_rows = level_rows[:cross_start] + [shaped[index] for index in range(LEVELS - cross_start)]
    state = coeff
    for level in range(LEVELS):
        bit = first_bit + level
        if bit < local_bits:
            other = paired(state, bit)
        else:
            if level == cross_start:
                state = regroup(state, groups)
            other = paired(state, bit - group_bits)
        state = level_product(level_rows[level], state, other)
    state = restore(state, groups)
    return state


def solution(mesh):
    return jax.shard_map(
        body,
        mesh=mesh,
        in_specs=(P("space", None, "exc"), P(None, "space", "exc", None)),
        out_specs=P("space", None, "exc"),
        check_vma=False,
    )
```

profile of v0, /device:TPU:0, one launch (start us, length us, event | category | flops | bytes accessed | tf_op | source)
XLA Modules:
  0.0 523.2 jit_solution(10234973929096856032)
XLA Ops:
  6.5 0.0 slice-start
  6.5 0.0 all-gather.11.cloned.1.call-start
  6.5 3.3 fusion.22
  9.8 0.0 all-gather.11.cloned.1.call-update
  9.9 0.0 all-gather.13.cloned.1.call-start
  9.9 0.7 all-gather.13.cloned.1.call-update
  10.6 0.0 all-gather.7.cloned.1.call-start
  10.7 0.0 slice-done
  10.7 0.2 copy.16
  10.9 30.4 %all_to_all.15 = f32[2,4,4,32,512]{4,3,2,0,1:T(8,128)S(1)} all-to-all(f32[2,4,4,32,512]{4,3,2,0,1:T(8,128)S(1)} %copy.16), channel_id=1, replica_groups=mesh['space'=4,'exc'=8] {'space'}, dimensions={1} | all-to-all | bytes 4194304 | tf_op jit(solution)/shard_map/all_to_all | solution.py:58
  41.3 1.6 fusion.23
  42.8 0.0 all-gather.7.cloned.1.call-update
  42.8 0.0 all-gather.9.cloned.1.call-start
  42.9 0.5 all-gather.9.cloned.1.call-update
  43.4 8.3 %rev.12 = f32[2,2,4,256,512]{4,3,2,1,0:T(8,128)} reverse(f32[2,2,4,256,512]{4,3,2,1,0:T(8,128)} %bitcast.36), dimensions={1} | reverse | bytes 16777216 | tf_op jit(solution)/shard_map/rev | solution.py:14
  51.7 43.1 %all-gather.11.cloned.1.call-done = f32[1,16,256,512]{3,2,1,0:T(8,128)} async-done(((f32[1,16,32,512]{3,2,1,0:T(8,128)}), f32[1,16,256,512]{3,2,1,0:T(8,128)}) %all-gather.11.cloned.1.call-update) | async-done | bytes 8388624 | tf_op jit(solution)/shard_map/all_gather | solution.py:29
  94.8 22.3 %fusion = f32[16,512,256]{1,2,0:T(8,128)} fusion(f32[16,256,512]{2,1,0:T(8,128)} %bitcast.41, f32[16,256,512]{2,1,0:T(8,128)} %param.2, f32[1,16,256,512]{3,2,1,0:T(8,128)} %all-gather.11.cloned.1.call-done), kind=kOutput, calls=%fused_computation | convolution fusion | flops 12889096192 | bytes 33554432 | tf_op jit(solution)/shard_map/brk,bke->bre/dot_general | solution.py:19
  117.1 8.1 %rev.13 = f32[1,2,8,256,512]{4,3,2,1,0:T(8,128)} reverse(f32[1,2,8,256,512]{4,3,2,1,0:T(8,128)} %bitcast.34), dimensions={1} | reverse | bytes 16777216 | tf_op jit(solution)/shard_map/rev | solution.py:14
  125.2 51.7 %all-gather.13.cloned.1.call-done = f32[1,16,256,512]{3,2,1,0:T(8,128)} async-done(((f32[1,16,32,512]{3,2,1,0:T(8,128)}), f32[1,16,256,512]{3,2,1,0:T(8,128)}) %all-gather.13.cloned.1.call-update) | async-done | bytes 8388624 | tf_op jit(solution)/shard_map/all_gather | solution.py:29
  176.9 35.8 %fusion.4 = f32[16,512,256]{2,1,0:T(8,128)} fusion(f32[16,256,512]{2,1,0:T(8,128)} %bitcast.39, f32[16,256,512]{2,1,0:T(8,128)} %bitcast.35, f32[1,16,256,512]{3,2,1,0:T(8,128)} %all-gather.13.cloned.1.call-done), kind=kOutput, calls=%fused_computation.4 | convolution fusion | flops 12889096192 | bytes 33554432 | tf_op jit(solution)/shard_map/brk,bke->bre/dot_general | solution.py:19
  212.7 101.0 %all_to_all.16 = f32[4,4,256,512]{2,3,1,0:T(8,128)} all-to-all(f32[4,4,256,512]{2,3,1,0:T(8,128)} %bitcast.42), channel_id=1, replica_groups=mesh['space'=4,'exc'=8] {'space'}, dimensions={0} | all-to-all | bytes 16777216 | tf_op jit(solution)/shard_map/all_to_all | solution.py:34
  313.7 9.9 %copy.15 = f32[2,2,4,256,512]{4,3,2,1,0:T(8,128)} copy(f32[2,2,4,256,512]{3,4,2,1,0:T(8,128)} %bitcast.31) | data formatting | bytes 16777216 | tf_op jit(solution)/shard_map/reshape;reshape | solution.py:13
  323.5 8.0 %rev.14 = f32[2,2,4,256,512]{4,3,2,1,0:T(8,128)} reverse(f32[2,2,4,256,512]{4,3,2,1,0:T(8,128)} %copy.15), dimensions={1} | reverse | bytes 16777216 | tf_op jit(solution)/shard_map/rev | solution.py:14
  331.6 9.9 %copy.14 = f32[4,4,256,512]{3,2,1,0:T(8,128)} copy(f32[4,4,256,512]{2,3,1,0:T(8,128)} %all_to_all.16) | data formatting | bytes 16777216 | tf_op jit(solution)/shard_map/all_to_all | solution.py:34
  341.5 0.0 all-gather.7.cloned.1.call-done
  341.5 21.6 %fusion.8 = f32[16,512,256]{1,2,0:T(8,128)} fusion(f32[16,256,512]{2,1,0:T(8,128)} %all-gather.7.cloned.1.call-done, f32[16,256,512]{2,1,0:T(8,128)} %bitcast.37, f32[16,256,512]{2,1,0:T(8,128)} %bitcast.38), kind=kOutput, calls=%fused_computation.8 | convolution fusion | flops 12889096192 | bytes 33554432 | tf_op jit(solution)/shard_map/brk,bke->bre/dot_general | solution.py:19
  363.1 8.1 %rev.15 = f32[1,2,8,256,512]{4,3,2,1,0:T(8,128)} reverse(f32[1,2,8,256,512]{4,3,2,1,0:T(8,128)} %bitcast.32), dimensions={1} | reverse | bytes 16777216 | tf_op jit(solution)/shard_map/rev | solution.py:14
  371.2 0.0 all-gather.9.cloned.1.call-done
  371.2 35.4 %fusion.12 = f32[16,512,256]{2,1,0:T(8,128)} fusion(f32[16,256,512]{2,1,0:T(8,128)} %all-gather.9.cloned.1.call-done, f32[16,256,512]{2,1,0:T(8,128)} %bitcast.40, f32[16,256,512]{2,1,0:T(8,128)} %bitcast.33), kind=kOutput, calls=%fused_computation.12 | convolution fusion | flops 12889096192 | bytes 33554432 | tf_op jit(solution)/shard_map/brk,bke->bre/dot_general | solution.py:19
  406.6 99.8 %all_to_all.17 = f32[4,4,256,512]{2,3,1,0:T(8,128)} all-to-all(f32[4,4,256,512]{2,3,1,0:T(8,128)} %bitcast.43), channel_id=1, replica_groups=mesh['space'=4,'exc'=8] {'space'}, dimensions={0} | all-to-all | bytes 16777216 | tf_op jit(solution)/shard_map/all_to_all | solution.py:41
  506.4 9.9 %copy.18 = f32[4,4,256,512]{3,2,1,0:T(8,128)} copy(f32[4,4,256,512]{2,3,1,0:T(8,128)} %all_to_all.17) | data formatting | bytes 16777216 | tf_op jit(solution)/shard_map/all_to_all | solution.py:41
Async XLA Ops:
  6.5 4.1 slice-start
  6.5 88.2 %all-gather.11.cloned.1.call-start = ((), (), s32[]{:S(2)}) async-start(), calls=%async_computation.5 | async-start | bytes 9437184 | tf_op jit(solution)/shard_map/all_gather | solution.py:29
  9.9 167.1 %all-gather.13.cloned.1.call-start = ((), (), s32[]{:S(2)}) async-start(), calls=%async_computation.6 | async-start | bytes 9437184 | tf_op jit(solution)/shard_map/all_gather | solution.py:29
  10.6 330.9 %all-gather.7.cloned.1.call-start = ((), (), s32[]{:S(2)}) async-start(), calls=%async_computation.3 | async-start | bytes 9437184 | tf_op jit(solution)/shard_map/all_gather | solution.py:29
  42.8 328.4 %all-gather.9.cloned.1.call-start = ((), (), s32[]{:S(2)}) async-start(), calls=%async_computation.4 | async-start | bytes 9437184 | tf_op jit(solution)/shard_map/all_gather | solution.py:29
Sparse Core Ops, SparseCore 0:
  10.0 84.7 all-gather.10
  96.4 80.5 all-gather.12
  178.5 80.5 all-gather.6
  260.6 80.5 all-gather.8
where the time goes:
time: 530 us; the launch traced here: 523 us
  blocking collectives  231 us (44%)
  matrix products  115 us (22%)
  waiting for transfers between devices  96.1 us (18%)
  local copies, waits for them, and re-layouts  67.3 us (13%)
  between operations  13.5 us (3%)
    dot_general x4, matrix products, contract(): jnp.einsum('brk,bke->bre', rows, stacked, precision=lax.Precision.HIGHEST...  115 us
    all_to_all x1, blocking collectives, regroup(): lax.all_to_all(shaped, 'space', split_axis=0, concat_axis=0, tiled=True)  101 us
    all_to_all x1, blocking collectives, restore(): lax.all_to_all(shaped, 'space', split_axis=0, concat_axis=0, tiled=True)  99.8 us
    all_gather x4, waiting for transfers between devices, level_product(): lax.all_gather(rows_dev, 'exc', axis=1, tiled=True)  94.8 us
    rev x4, local copies, waits for them, and re-layouts, paired(): return shaped[:, ::-1].reshape(state.shape)  32.5 us
    all_to_all x1, blocking collectives, body(): lax.all_to_all(shaped, 'space', split_axis=1, concat_axis=1, tiled=True)  30.4 us
  transfers between devices with their start and end apart: 4, of which 2 were waited for; matrix products, arithmetic and copies ran while one was open for 26% of the time, Pallas kernels for 0%

commit v1 on v0

--- a/solution.py
+++ b/solution.py
@@ -1,10 +1,22 @@
+import functools
 import jax
 import jax.numpy as jnp
 from jax import lax
 from jax.sharding import PartitionSpec as P
+from jax.lax import all_to_all, axis_size
 
 BITS = 6
 LEVELS = 4
+
+
+def _refer_map(obj, axis_key):
+    plain = jnp.stack(jnp.split(obj, axis_size(axis_key), axis=1), 0)
+    right_arr = all_to_all(plain, axis_name=axis_key, split_axis=0, concat_axis=0)
+    seen_now = jnp.concatenate(right_arr, axis=1)
+    return seen_now
+
+
+attach_tiles = functools.partial(_refer_map, axis_key="space")
 
 
 def paired(state, bit):
@@ -55,9 +67,7 @@
     shaped = moved.reshape(
         moved.shape[0], groups, blocks_dev // groups, moved.shape[2], moved.shape[3]
     )
-    shaped = lax.all_to_all(shaped, "space", split_axis=1, concat_axis=1, tiled=True).reshape(
-        moved.shape
-    )
+    shaped = attach_tiles(shaped).reshape(moved.shape)
     level_rows = level_rows[:cross_start] + [shaped[index] for index in range(LEVELS - cross_start)]
     state = coeff
     for level in range(LEVELS):

time: 530 us -> 499 us (0.942); the launches traced: 523 us -> 498 us
  matrix products: 115 us -> 100 us
  local copies, waits for them, and re-layouts: 67.3 us -> 60.8 us
    dot_general x4, matrix products: 115 us -> 100 us  [contract(): jnp.einsum('brk,bke->bre', rows, stacked, precision=lax.Precision.HIGHEST...]
    all_to_all x1 -> x0, local copies, waits for them, and re-layouts: 9.87 us -> none  [restore(): lax.all_to_all(shaped, 'space', split_axis=0, concat_axis=0, tiled=True)]
  transfers between devices with their start and end apart: 4 -> 4, of which waited for: 2 -> 2; matrix products, arithmetic and copies ran while one was open for 26% -> 27% of each run, Pallas kernels for 0% -> 0%
where the time goes in v1:
time: 499 us; the launch traced here: 498 us
  blocking collectives  228 us (46%)
  matrix products  100 us (20%)
  waiting for transfers between devices  95.8 us (19%)
  local copies, waits for them, and re-layouts  60.8 us (12%)
  between operations  13.2 us (3%)
    all_to_all x1, blocking collectives, regroup(): lax.all_to_all(shaped, 'space', split_axis=0, concat_axis=0, tiled=True)  101 us
    dot_general x4, matrix products, contract(): jnp.einsum('brk,bke->bre', rows, stacked, precision=lax.Precision.HIGHEST...  100 us
    all_to_all x1, blocking collectives, restore(): lax.all_to_all(shaped, 'space', split_axis=0, concat_axis=0, tiled=True)  96.3 us
    all_gather x4, waiting for transfers between devices, level_product(): lax.all_gather(rows_dev, 'exc', axis=1, tiled=True)  94.6 us
    rev x4, local copies, waits for them, and re-layouts, paired(): return shaped[:, ::-1].reshape(state.shape)  32.5 us
    all_to_all x1, blocking collectives, _refer_map(): all_to_all(plain, axis_name=axis_key, split_axis=0, concat_axis=0)  30.4 us
  transfers between devices with their start and end apart: 4, of which 2 were waited for; matrix products, arithmetic and copies ran while one was open for 27% of the time, Pallas kernels for 0%

profile of v1, /device:TPU:0, one launch (start us, length us, event | category | flops | bytes accessed | tf_op | source)
XLA Modules:
  0.0 498.1 jit_solution(5611487796487392587)
XLA Ops:
  6.5 0.0 slice-start
  6.5 0.0 all-gather.11.cloned.1.call-start
  6.5 3.3 fusion.22
  9.8 0.0 all-gather.11.cloned.1.call-update
  9.9 0.0 all-gather.13.cloned.1.call-start
  9.9 0.7 all-gather.13.cloned.1.call-update
  10.6 0.0 all-gather.9.cloned.1.call-start
  10.7 0.0 slice-done
  10.7 0.2 slice_bitcast_fusion.3
  10.9 0.3 maximum_bitcast_fusion
  11.2 30.4 %all_to_all.15 = f32[4,2,1,4,32,512]{5,4,3,2,1,0:T(8,128)S(1)} all-to-all(f32[4,2,1,4,32,512]{5,4,3,2,1,0:T(8,128)S(1)} %maximum_bitcast_fusion), channel_id=1, replica_groups=mesh['space'=4,'exc'=8] {'space'}, dimensions={0} | all-to-all | bytes 4194304 | tf_op jit(solution)/shard_map/all_to_all | solution.py:14
  41.5 1.5 fusion.23
  43.1 0.0 all-gather.9.cloned.1.call-update
  43.1 0.0 all-gather.7.cloned.1.call-start
  43.2 0.5 all-gather.7.cloned.1.call-update
  43.7 8.2 %rev.12 = f32[2,2,4,256,512]{4,3,2,1,0:T(8,128)} reverse(f32[2,2,4,256,512]{4,3,2,1,0:T(8,128)} %bitcast.49), dimensions={1} | reverse | bytes 16777216 | tf_op jit(solution)/shard_map/rev | solution.py:26
  51.9 42.8 %all-gather.11.cloned.1.call-done = f32[1,16,256,512]{3,2,1,0:T(8,128)} async-done(((f32[1,16,32,512]{3,2,1,0:T(8,128)}), f32[1,16,256,512]{3,2,1,0:T(8,128)}) %all-gather.11.cloned.1.call-update) | async-done | bytes 8388624 | tf_op jit(solution)/shard_map/all_gather | solution.py:41
  94.8 22.3 %fusion = f32[16,512,256]{1,2,0:T(8,128)} fusion(f32[16,256,512]{2,1,0:T(8,128)} %bitcast.54, f32[16,256,512]{2,1,0:T(8,128)} %param.2, f32[1,16,256,512]{3,2,1,0:T(8,128)} %all-gather.11.cloned.1.call-done), kind=kOutput, calls=%fused_computation | convolution fusion | flops 12889096192 | bytes 33554432 | tf_op jit(solution)/shard_map/brk,bke->bre/dot_general | solution.py:31
  117.1 8.1 %rev.13 = f32[1,2,8,256,512]{4,3,2,1,0:T(8,128)} reverse(f32[1,2,8,256,512]{4,3,2,1,0:T(8,128)} %bitcast.46), dimensions={1} | reverse | bytes 16777216 | tf_op jit(solution)/shard_map/rev | solution.py:26
  125.2 51.7 %all-gather.13.cloned.1.call-done = f32[1,16,256,512]{3,2,1,0:T(8,128)} async-done(((f32[1,16,32,512]{3,2,1,0:T(8,128)}), f32[1,16,256,512]{3,2,1,0:T(8,128)}) %all-gather.13.cloned.1.call-update) | async-done | bytes 8388624 | tf_op jit(solution)/shard_map/all_gather | solution.py:41
  176.9 35.5 %fusion.4 = f32[16,512,256]{2,1,0:T(8,128)} fusion(f32[16,256,512]{2,1,0:T(8,128)} %bitcast.52, f32[16,256,512]{2,1,0:T(8,128)} %bitcast.47, f32[1,16,256,512]{3,2,1,0:T(8,128)} %all-gather.13.cloned.1.call-done), kind=kOutput, calls=%fused_computation.4 | convolution fusion | flops 12889096192 | bytes 33554432 | tf_op jit(solution)/shard_map/brk,bke->bre/dot_general | solution.py:31
  212.4 100.9 %all_to_all.16 = f32[4,4,256,512]{2,3,1,0:T(8,128)} all-to-all(f32[4,4,256,512]{2,3,1,0:T(8,128)} %bitcast.55), channel_id=1, replica_groups=mesh['space'=4,'exc'=8] {'space'}, dimensions={0} | all-to-all | bytes 16777216 | tf_op jit(solution)/shard_map/all_to_all | solution.py:46
  313.3 9.9 %copy.22 = f32[2,2,4,256,512]{4,3,2,1,0:T(8,128)} copy(f32[2,2,4,256,512]{3,4,2,1,0:T(8,128)} %bitcast.44) | data formatting | bytes 16777216 | tf_op jit(solution)/shard_map/reshape;reshape | solution.py:25
  323.3 8.0 %rev.14 = f32[2,2,4,256,512]{4,3,2,1,0:T(8,128)} reverse(f32[2,2,4,256,512]{4,3,2,1,0:T(8,128)} %copy.22), dimensions={1} | reverse | bytes 16777216 | tf_op jit(solution)/shard_map/rev | solution.py:26
  331.3 9.9 %copy.21 = f32[4,4,256,512]{3,2,1,0:T(8,128)} copy(f32[4,4,256,512]{2,3,1,0:T(8,128)} %all_to_all.16) | data formatting | bytes 16777216 | tf_op jit(solution)/shard_map/all_to_all | solution.py:46
  341.2 0.0 all-gather.9.cloned.1.call-done
  341.2 21.2 %fusion.8 = f32[16,256,512]{2,1,0:T(8,128)} fusion(f32[16,256,512]{2,1,0:T(8,128)} %all-gather.9.cloned.1.call-done, f32[16,256,512]{2,1,0:T(8,128)} %bitcast.50, f32[16,256,512]{2,1,0:T(8,128)} %bitcast.51), kind=kOutput, calls=%fused_computation.8 | convolution fusion | flops 12889096192 | bytes 33554432 | tf_op jit(solution)/shard_map/brk,bke->bre/dot_general | solution.py:31
  362.4 8.1 %rev.15 = f32[1,2,8,256,512]{4,3,2,1,0:T(8,128)} reverse(f32[1,2,8,256,512]{4,3,2,1,0:T(8,128)} %bitcast.45), dimensions={1} | reverse | bytes 16777216 | tf_op jit(solution)/shard_map/rev | solution.py:26
  370.6 0.0 all-gather.7.cloned.1.call-done
  370.6 21.2 %fusion.12 = f32[16,256,512]{2,1,0:T(8,128)} fusion(f32[16,256,512]{2,1,0:T(8,128)} %all-gather.7.cloned.1.call-done, f32[16,256,512]{2,1,0:T(8,128)} %bitcast.53, f32[16,256,512]{2,1,0:T(8,128)} %fusion.8), kind=kOutput, calls=%fused_computation.12 | convolution fusion | flops 12889096192 | bytes 33554432 | tf_op jit(solution)/shard_map/brk,bke->bre/dot_general | solution.py:31
  391.8 96.3 %all_to_all.17 = f32[4,4,256,512]{3,2,1,0:T(8,128)S(1)} all-to-all(f32[4,4,256,512]{3,2,1,0:T(8,128)} %bitcast.56), channel_id=1, replica_groups=mesh['space'=4,'exc'=8] {'space'}, dimensions={0} | all-to-all | bytes 16777216 | tf_op jit(solution)/shard_map/all_to_all | solution.py:53
  488.1 3.4 copy.28
Async XLA Ops:
  6.5 4.1 slice-start
  6.5 88.2 %all-gather.11.cloned.1.call-start = ((), (), s32[]{:S(2)}) async-start(), calls=%async_computation.5 | async-start | bytes 9437184 | tf_op jit(solution)/shard_map/all_gather | solution.py:41
  9.9 167.1 %all-gather.13.cloned.1.call-start = ((), (), s32[]{:S(2)}) async-start(), calls=%async_computation.6 | async-start | bytes 9437184 | tf_op jit(solution)/shard_map/all_gather | solution.py:41
  10.6 330.6 %all-gather.9.cloned.1.call-start = ((), (), s32[]{:S(2)}) async-start(), calls=%async_computation.4 | async-start | bytes 9437184 | tf_op jit(solution)/shard_map/all_gather | solution.py:41
  43.1 327.4 %all-gather.7.cloned.1.call-start = ((), (), s32[]{:S(2)}) async-start(), calls=%async_computation.3 | async-start | bytes 9437184 | tf_op jit(solution)/shard_map/all_gather | solution.py:41
Sparse Core Ops, SparseCore 0:
  10.0 84.7 all-gather.10
  96.4 80.5 all-gather.12
  178.5 80.5 all-gather.8
  260.5 80.5 all-gather.6
